TPU v7x, 32 devices: a whole 2x2x4 slice. The times are simulated.
32 devices in a mesh: parts: 2 (over y), gy: 8 (over z, x), gz: 2 (over core).
Axes of the slice: x: 2, y: 2, z: 4, core: 2. Of those that a mesh axis runs over, the one named last changes fastest.
Arguments:
- volume: float32 [512, 16, 512], P('parts', 'gy', 'gz'), parts along dimension 0, may hold values from -96 to 96
- sigma_fine: float32 [3], replicated, may hold values from 0.8 to 2
- sigma_coarse: float32 [3], replicated, may hold values from 2.5 to 4
Outputs:
- dog: float32 [256, 8, 256], P('parts', 'gy', 'gz'), parts along dimension 0
There are 2 independent parts, one for each index of `parts`. A program takes and returns all parts, laid end to end along the dimension named above; an argument that names none is the same for every part. Nothing has to cross between parts.
All inputs are finite; a program needn't handle non-finite values.
Results may differ from a plain program's by a relative error of at most 0.0001.
Values sent between devices are 32-bit elements; how exact they have to be, the bound alone decides.
A program may use at most 64 MiB of HBM per device.

v0:
```python
import jax
import jax.numpy as jnp
from jax import lax
from jax.sharding import PartitionSpec as P

RADIUS = 30


def with_halo(cells, sides, width):
    for axis, dim in sides:
        count = lax.axis_size(axis)
        ends = count - 1
        head = lax.slice_in_dim(cells, 0, width, axis=dim)
        tail = lax.slice_in_dim(cells, cells.shape[dim] - width, cells.shape[dim], axis=dim)
        cells = jnp.concatenate(
            [
                lax.ppermute(tail, axis, [(i, (i + 1) % count) for i in range(ends)]),
                cells,
                lax.ppermute(head, axis, [((i + 1) % count, i) for i in range(ends)]),
            ],
            axis=dim,
        )
    return cells


def band_matrix(sigma_fine, sigma_coarse, axis_number, out_count, in_count, shift):
    offsets = jnp.arange(-RADIUS, RADIUS + 1).astype(jnp.float32)
    outputs = lax.broadcasted_iota(jnp.int32, (out_count, in_count), 0)
    inputs = lax.broadcasted_iota(jnp.int32, (out_count, in_count), 1)
    distance = inputs - shift - 2 * outputs
    inside = jnp.abs(distance) <= RADIUS
    spread = distance.astype(jnp.float32)
    mats = []
    for sigma in (sigma_fine[axis_number], sigma_coarse[axis_number]):
        total = jnp.sum(jnp.exp(-offsets * offsets / (2.0 * sigma * sigma)))
        values = jnp.exp(-spread * spread / (2.0 * sigma * sigma)) / total
        mats.append(jnp.where(inside, values, jnp.float32(0.0)))
    return jnp.stack(mats)


def along_last(field, matrix):
    return jnp.einsum(
        "sxyj,soj->sxyo",
        field,
        matrix,
        precision=lax.Precision.HIGHEST,
        preferred_element_type=jnp.float32,
    )


def along_rows(field, matrix):
    return jnp.einsum(
        "sxiz,soi->sxoz",
        field,
        matrix,
        precision=lax.Precision.HIGHEST,
        preferred_element_type=jnp.float32,
    )


def on_device(volume, sigma_fine, sigma_coarse):
    x_count = volume.shape[0]
    matrix_x = band_matrix(sigma_fine, sigma_coarse, 0, x_count // 2, x_count, 0)
    scaled = jnp.einsum(
        "soi,iyz->soyz",
        matrix_x,
        volume,
        precision=lax.Precision.HIGHEST,
        preferred_element_type=jnp.float32,
    )
    z_block = scaled.shape[3]
    rimmed = with_halo(scaled, (("gz", 3),), RADIUS)
    matrix_z = band_matrix(sigma_fine, sigma_coarse, 2, z_block // 2, rimmed.shape[3], RADIUS)
    scaled = along_last(rimmed, matrix_z)
    columns = lax.all_to_all(scaled, "gy", split_axis=1, concat_axis=2, tiled=True)
    y_whole = columns.shape[2]
    columns = along_rows(
        columns, band_matrix(sigma_fine, sigma_coarse, 1, y_whole // 2, y_whole, 0)
    )
    result = lax.all_to_all(columns[0] - columns[1], "gy", split_axis=1, concat_axis=0, tiled=True)
    return result


def solution(mesh):
    placed = (P("parts", "gy", "gz"), P(), P())
    return jax.shard_map(
        on_device, mesh=mesh, in_specs=placed, out_specs=P("parts", "gy", "gz"), check_vma=False
    )
```

profile of v0, /device:TPU:0, one launch (start us, length us, event | category | flops | bytes accessed | tf_op | source)
XLA Modules:
  0.0 46.8 jit_solution(1939435119756216192)
XLA Ops:
  0.0 0.6 %copy-done = f32[3]{0:T(128)S(1)} copy-done((f32[3]{0:T(128)S(1)}, f32[3]{0:T(128)}, u32[]{:S(2)}) %copy-start) | copy-done | bytes 36
  0.7 0.7 %fusion.29 = (f32[1]{0:T(128)}, f32[1]{0:T(128)}, f32[1]{0:T(128)}) fusion(f32[3]{0:T(128)S(1)} %copy-done), kind=kLoop, calls=%fused_computation.57 | loop fusion | bytes 24 | tf_op jit(solution)/shard_map/slice | solution.py:34
  2.0 0.0 copy-start.1
  2.7 0.6 %fusion.30 = (f32[1]{0:T(128)}, f32[1]{0:T(128)}, f32[1]{0:T(128)}) fusion(f32[3]{0:T(128)S(1)} %copy-done.1), kind=kLoop, calls=%fused_computation.58 | loop fusion | bytes 24 | tf_op jit(solution)/shard_map/slice | solution.py:34
  4.5 0.7 %exponential_reduce_fusion.2 = (f32[]{:T(128)}, f32[]{:T(128)}) fusion(f32[]{:T(128)S(6)} %mul.168, f32[]{:T(128)S(6)} %mul.166), kind=kLoop, calls=%fused_computation.47 | loop fusion | flops 486 | bytes 16 | tf_op jit(solution)/shard_map/reduce_sum | solution.py:35
  5.2 1.4 %divide_select_fusion.1 = (f32[1,128,256]{2,1,0:T(8,128)S(1)}, f32[1,128,256]{2,1,0:T(8,128)S(1)}) fusion(f32[]{:T(128)} %get-tuple-element.20, f32[]{:T(128)S(6)} %mul.166, s32[128]{0:T(128)S(1)} %iota_multiply_fusion, f32[]{:T(128)} %get-tuple-element.19, f32[]{:T(128)S(6)} %mul.168), kind=kLoop, calls=%fused_computation.30 | loop fusion | flops 393216 | bytes 262672 | tf_op jit(solution)/shard_map/jit(_where)/select_n | solution.py:37
  6.6 1.7 %fusion.6 = f32[2,128,2,256]{3,1,2,0:T(8,128)S(1)} fusion(f32[256,2,256]{2,1,0:T(2,128)} %param.3, f32[1,128,256]{2,1,0:T(8,128)S(1)} %get-tuple-element.18, f32[1,128,256]{2,1,0:T(8,128)S(1)} %get-tuple-element.17), kind=kOutput, calls=%fused_computation.7 | convolution fusion | flops 402718720 | bytes 1310720 | tf_op jit(solution)/shard_map/soi,iyz->soyz/dot_general | solution.py:64
  8.3 0.1 fusion.28
  8.4 2.4 %collective-permute-start = (f32[2,128,2,30]{3,1,2,0:T(8,128)S(1)}, f32[2,128,2,30]{3,1,2,0:T(8,128)S(1)}, u32[]{:S(2)}, u32[]{:S(2)}) collective-permute-start(f32[2,128,2,30]{3,1,2,0:T(8,128)S(1)} %get-tuple-element.5), channel_id=1, source_target_pairs={{0,1},{2,3},{4,5},{6,7},{8,9},{10,11},{12,13},{14,15},{16,17},{18,... | collective-permute-start | bytes 184328 | tf_op jit(solution)/shard_map/ppermute | solution.py:17
  10.9 1.3 %collective-permute-start.1 = (f32[2,128,2,30]{3,1,2,0:T(8,128)S(1)}, f32[2,128,2,30]{3,1,2,0:T(8,128)S(1)}, u32[]{:S(2)}, u32[]{:S(2)}) collective-permute-start(f32[2,128,2,30]{3,1,2,0:T(8,128)S(1)} %get-tuple-element.6), channel_id=1, source_target_pairs={{1,0},{3,2},{5,4},{7,6},{9,8},{11,10},{13,12},{15,14},{17,16},{19,... | collective-permute-start | bytes 184328 | tf_op jit(solution)/shard_map/ppermute | solution.py:19
  14.7 0.7 %exponential_reduce_fusion = (f32[]{:T(128)}, f32[]{:T(128)}) fusion(f32[]{:T(128)S(6)} %mul.173, f32[]{:T(128)S(6)} %mul.171), kind=kLoop, calls=%fused_computation.45 | loop fusion | flops 486 | bytes 16 | tf_op jit(solution)/shard_map/reduce_sum | solution.py:35
  15.4 1.4 %fusion.18 = (f32[1,128,316]{1,2,0:T(8,128)S(1)}, f32[1,128,316]{1,2,0:T(8,128)S(1)}) fusion(f32[]{:T(128)} %get-tuple-element.22, f32[]{:T(128)S(6)} %mul.171, s32[128]{0:T(128)S(1)} %iota_multiply_fusion, s32[316]{0:T(512)S(1)} %iota_add_fusion, f32[]{:T(128)} %get-tuple-element.21, f32[]{:T(128)S(6)} %mul.173), kind=kLoop, calls=%fused_computation.25 | loop fusion | flops 485376 | bytes 325376 | tf_op jit(solution)/shard_map/jit(_where)/select_n | solution.py:37
  16.8 0.0 collective-permute-done
  16.8 0.0 collective-permute-done.1
  16.8 1.0 %fusion = f32[2,128,2,128]{3,1,2,0:T(8,128)S(1)} fusion(f32[2,128,2,30]{3,1,2,0:T(8,128)S(1)} %collective-permute-done.1, f32[2,128,2,256]{3,1,2,0:T(8,128)S(1)} %fusion.6, f32[2,128,2,30]{3,1,2,0:T(8,128)S(1)} %collective-permute-done, f32[1,128,316]{1,2,0:T(8,128)S(1)} %get-tuple-element.8, f32[1,128,316]{1,2,0:T(8,128)S(1)} %get-tuple-element.7), kind=kOutput, calls=%fused_computation.1 | convolution fusion | flops 248916992 | bytes 1232896 | tf_op jit(solution)/shard_map/sxyj,soj->sxyo/dot_general | solution.py:42
  17.8 0.9 %copy.14 = f32[2,128,2,128]{3,2,0,1:T(2,128)} copy(f32[2,128,2,128]{3,1,2,0:T(8,128)S(1)} %fusion) | data formatting | bytes 524288 | tf_op jit(solution)/shard_map/sxyj,soj->sxyo/dot_general | solution.py:42
  18.7 6.6 %all-to-all-start = ((f32[2,128,2,128]{3,2,0,1:T(2,128)}), f32[2,128,2,128]{3,2,0,1:T(2,128)S(1)}, u32[]{:S(2)}, u32[]{:S(2)}) async-start(f32[2,128,2,128]{3,2,0,1:T(2,128)} %copy.14), calls=%async_computation | async-start | bytes 524288 | tf_op jit(solution)/shard_map/all_to_all | solution.py:75
  27.8 0.7 %exponential_reduce_fusion.4 = (f32[]{:T(128)}, f32[]{:T(128)}) fusion(f32[]{:T(128)S(6)} %mul.161, f32[]{:T(128)S(6)} %mul.158), kind=kLoop, calls=%fused_computation.50 | loop fusion | flops 486 | bytes 16 | tf_op jit(solution)/shard_map/reduce_sum | solution.py:35
  28.5 1.3 %divide_select_fusion.3 = (f32[1,8,16]{2,1,0:T(8,128)S(1)}, f32[1,8,16]{2,1,0:T(8,128)S(1)}) fusion(f32[]{:T(128)} %get-tuple-element.24, f32[]{:T(128)S(6)} %mul.158, s32[8]{0:T(128)S(1)} %iota_multiply_fusion.1, f32[]{:T(128)} %get-tuple-element.23, f32[]{:T(128)S(6)} %mul.161), kind=kLoop, calls=%fused_computation.40 | loop fusion | flops 1536 | bytes 1072 | tf_op jit(solution)/shard_map/jit(_where)/select_n | solution.py:37
  29.9 5.6 %all-to-all-done = f32[2,128,2,128]{3,2,0,1:T(2,128)S(1)} async-done(((f32[2,128,2,128]{3,2,0,1:T(2,128)}), f32[2,128,2,128]{3,2,0,1:T(2,128)S(1)}, u32[]{:S(2)}, u32[]{:S(2)}) %all-to-all-start) | async-done | bytes 262176 | tf_op jit(solution)/shard_map/all_to_all | solution.py:75
  35.5 0.1 copy.15
  35.6 0.3 convolution_bitcast_fusion
  35.9 10.3 %all_to_all.36 = f32[16,8,128]{2,0,1:T(8,128)S(1)} all-to-all(f32[16,8,128]{2,0,1:T(8,128)S(1)} %copy.16), channel_id=1, replica_groups=mesh['parts'=2,'gy'=8,'gz'=2] {'gy'}, dimensions={1} | all-to-all | bytes 131072 | tf_op jit(solution)/shard_map/all_to_all | solution.py:80
  46.2 0.6 %copy.27 = f32[128,1,128]{2,1,0:T(1,128)} copy(f32[128,1,128]{2,1,0:T(1,128)S(1)} %bitcast.42) | data formatting | bytes 131072
  (7 shorter events, 0.0 us)
Async XLA Ops:
  0.0 0.7 %copy-start = (f32[3]{0:T(128)S(1)}, f32[3]{0:T(128)}, u32[]{:S(2)}) copy-start(f32[3]{0:T(128)} %param.4) | copy-start | bytes 40
  2.0 0.7 %copy-start.1 = (f32[3]{0:T(128)S(1)}, f32[3]{0:T(128)}, u32[]{:S(2)}) copy-start(f32[3]{0:T(128)} %param.5) | copy-start | bytes 40
  8.4 8.3 %collective-permute-start = (f32[2,128,2,30]{3,1,2,0:T(8,128)S(1)}, f32[2,128,2,30]{3,1,2,0:T(8,128)S(1)}, u32[]{:S(2)}, u32[]{:S(2)}) collective-permute-start(f32[2,128,2,30]{3,1,2,0:T(8,128)S(1)} %get-tuple-element.5), channel_id=1, source_target_pairs={{0,1},{2,3},{4,5},{6,7},{8,9},{10,11},{12,13},{14,15},{16,17},{18,... | collective-permute-start | bytes 184328 | tf_op jit(solution)/shard_map/ppermute | solution.py:17
  10.9 5.9 %collective-permute-start.1 = (f32[2,128,2,30]{3,1,2,0:T(8,128)S(1)}, f32[2,128,2,30]{3,1,2,0:T(8,128)S(1)}, u32[]{:S(2)}, u32[]{:S(2)}) collective-permute-start(f32[2,128,2,30]{3,1,2,0:T(8,128)S(1)} %get-tuple-element.6), channel_id=1, source_target_pairs={{1,0},{3,2},{5,4},{7,6},{9,8},{11,10},{13,12},{15,14},{17,16},{19,... | collective-permute-start | bytes 184328 | tf_op jit(solution)/shard_map/ppermute | solution.py:19
  18.7 16.8 %all-to-all-start = ((f32[2,128,2,128]{3,2,0,1:T(2,128)}), f32[2,128,2,128]{3,2,0,1:T(2,128)S(1)}, u32[]{:S(2)}, u32[]{:S(2)}) async-start(f32[2,128,2,128]{3,2,0,1:T(2,128)} %copy.14), calls=%async_computation | async-start | bytes 524288 | tf_op jit(solution)/shard_map/all_to_all | solution.py:75
where the time goes:
time: 47.3 us; the launch traced here: 46.8 us
  starting transfers between devices  10.3 us (22%)
  blocking collectives  10.3 us (22%)
  between operations  7.74 us (16%)
  other arithmetic  6.24 us (13%)
  waiting for transfers between devices  5.61 us (12%)
  local copies, waits for them, and re-layouts  3.69 us (8%)
  matrix products  2.88 us (6%)
    all_to_all x1, blocking collectives, on_device(): lax.all_to_all(columns[0] - columns[1], 'gy', split_axis=1, concat_axis=0...  10.3 us
    all_to_all x1, starting transfers between devices, on_device(): lax.all_to_all(scaled, 'gy', split_axis=1, concat_axis=2, tiled=True)  6.62 us
    all_to_all x1, waiting for transfers between devices, on_device(): lax.all_to_all(scaled, 'gy', split_axis=1, concat_axis=2, tiled=True)  5.61 us
    select_n x3, other arithmetic, band_matrix(): mats.append(jnp.where(inside, values, jnp.float32(0.0)))  4.16 us
    ppermute x1, starting transfers between devices, with_halo(): lax.ppermute(tail, axis, [(i, (i + 1) % count) for i in range(ends)])  2.41 us
    reduce_sum x3, other arithmetic, band_matrix(): total = jnp.sum(jnp.exp(-offsets * offsets / (2.0 * sigma * sigma)))  2.05 us
    dot_general x1, matrix products, on_device(): jnp.einsum('soi,iyz->soyz', matrix_x, volume, precision=lax.Precision.HIG...  1.66 us
    ppermute x1, starting transfers between devices, with_halo(): lax.ppermute(head, axis, [((i + 1) % count, i) for i in range(ends)])  1.29 us
  transfers between devices with their start and end apart: 3, of which 1 were waited for; matrix products, arithmetic and copies ran while one was open for 9% of the time, Pallas kernels for 0%

commit v1 on v0

v1 whole, which is shorter than its diff:
```python
import functools

import jax
import jax.numpy as jnp
from jax import lax
from jax.experimental import pallas as pl
from jax.experimental.pallas import tpu as pltpu
from jax.sharding import PartitionSpec as P

RADIUS = 30
LANES = 128
SUB = 8
CHUNKS = 4
PAIR = 2
MESH = pl.DeviceIdType.MESH


def dot(a, b):
    return jnp.dot(a, b, precision=lax.Precision.HIGHEST, preferred_element_type=jnp.float32)


def splat(value):
    return jnp.full((1, LANES), value, jnp.float32)


def tap_scale(sigma):
    s = splat(sigma)
    rate = 1.0 / (2.0 * s * s)
    t = (lax.broadcasted_iota(jnp.int32, (1, LANES), 1) - RADIUS).astype(jnp.float32)
    e = jnp.where(jnp.abs(t) <= RADIUS, jnp.exp(-(t * t) * rate), 0.0)
    return rate, 1.0 / jnp.broadcast_to(jnp.sum(e, axis=1, keepdims=True), (1, LANES))


def taps_at(distance, scale):
    rate, norm = scale
    d = distance.astype(jnp.float32)
    return jnp.where(jnp.abs(distance) <= RADIUS, jnp.exp(-(d * d) * rate) * norm, 0.0)


def kernel(
    groups, vol, sf, sc, out, vbuf, hbuf, wx, wz, zs, xsend, xrecv, psend, precv,
    load_sem, halo_sems, x_send_sems, x_recv_sems, p_send_sems, p_recv_sems,
):
    x_count, y_rows, z_count = vol.shape
    x_out, z_out = x_count // 2, z_count // 2
    rows = x_out // CHUNKS
    lines = groups // PAIR
    me = lax.axis_index("gy")
    core = lax.axis_index("gz")
    hi, lo = me // PAIR, me % PAIR
    mate = me + 1 - 2 * lo

    barrier = pltpu.get_barrier_semaphore()

    def hello(device):
        pl.semaphore_signal(barrier, inc=1, device_id=device, device_id_type=MESH)

    hello({"gz": 1 - core})
    hello({"gy": mate})
    for k in range(1, lines):
        hello({"gy": ((hi + k) % lines) * PAIR + lo})

    loads = [
        pltpu.make_async_copy(vol.at[:, y, :], vbuf.at[y], load_sem.at[y]) for y in range(y_rows)
    ]
    for load in loads:
        load.start()
    pl.semaphore_wait(barrier, 1 + 1 + (lines - 1))
    edge = pl.multiple_of((1 - core) * (z_count - LANES), LANES)
    halos = [
        pltpu.make_async_remote_copy(
            src_ref=vol.at[:, y, pl.ds(edge, LANES)],
            dst_ref=hbuf.at[y],
            send_sem=halo_sems.at[0, y],
            recv_sem=halo_sems.at[1, y],
            device_id={"gz": 1 - core},
            device_id_type=MESH,
        )
        for y in range(y_rows)
    ]
    for halo in halos:
        halo.start()

    scales = [[tap_scale(ref[a]) for ref in (sf, sc)] for a in range(3)]
    halo_first = z_count - (z_count + LANES) * core
    for s in range(2):
        i = lax.broadcasted_iota(jnp.int32, (z_count, z_out), 0)
        o = lax.broadcasted_iota(jnp.int32, (z_count, z_out), 1)
        wz[:z_count, s * z_out:(s + 1) * z_out] = taps_at(i - 2 * o, scales[2][s])
        i = lax.broadcasted_iota(jnp.int32, (LANES, z_out), 0) + halo_first
        o = lax.broadcasted_iota(jnp.int32, (LANES, z_out), 1)
        wz[z_count:, s * z_out:(s + 1) * z_out] = taps_at(i - 2 * o, scales[2][s])
        for b in range(x_count // LANES):
            o = lax.broadcasted_iota(jnp.int32, (x_out, LANES), 0)
            i = lax.broadcasted_iota(jnp.int32, (x_out, LANES), 1) + b * LANES
            wx[s, :, b * LANES:(b + 1) * LANES] = taps_at(i - 2 * o, scales[0][s])

    for y in range(y_rows):
        loads[y].wait()
        part = dot(vbuf[y], wz[:z_count, :])
        halos[y].wait_recv()
        part = part + dot(hbuf[y], wz[z_count:, :])
        for s in range(2):
            zs[s, :, y * z_out:(y + 1) * z_out] = part[:, s * z_out:(s + 1) * z_out]

    swaps = []
    for c in range(CHUNKS):
        for s in range(2):
            part = dot(wx[s, c * rows:(c + 1) * rows, :], zs[s])
            for y in range(y_rows):
                xsend[c, s * y_rows + y] = part[:, y * z_out:(y + 1) * z_out].reshape(
                    rows // SUB, SUB, z_out
                )
        swap = pltpu.make_async_remote_copy(
            src_ref=xsend.at[c],
            dst_ref=xrecv.at[c],
            send_sem=x_send_sems.at[c],
            recv_sem=x_recv_sems.at[c],
            device_id={"gy": mate},
            device_id_type=MESH,
        )
        swap.start()
        swaps.append(swap)

    def y_tap(s, row, target):
        d = jnp.full((SUB, LANES), row - 2 * target, jnp.int32)
        return taps_at(d, scales[1][s])[None]

    sign = (1.0, -1.0)
    targets = [((hi + k) % lines) * PAIR + lo for k in range(lines)]
    taps = []
    for target in targets:
        taps.append([
            [sign[s] * y_tap(s, owner * y_rows + y, target) for s in range(2) for y in range(y_rows)]
            for owner in (me, mate)
        ])

    order = list(range(1, lines)) + [0]
    pushes = []
    for c in range(CHUNKS):
        swaps[c].wait_recv()
        for k in order:
            total = None
            for held, row_taps in ((xsend, taps[k][0]), (xrecv, taps[k][1])):
                for j, tap in enumerate(row_taps):
                    term = tap * held[c, j]
                    total = term if total is None else total + term
            psend[c, k] = total
            if k:
                push = pltpu.make_async_remote_copy(
                    src_ref=psend.at[c, k],
                    dst_ref=precv.at[c, k],
                    send_sem=p_send_sems.at[c, k],
                    recv_sem=p_recv_sems.at[c, k],
                    device_id={"gy": targets[k]},
                    device_id_type=MESH,
                )
                push.start()
                pushes.append((c, push))

    for c in range(CHUNKS):
        total = psend[c, 0]
        mine = [push for chunk, push in pushes if chunk == c]
        for k, push in enumerate(mine, start=1):
            push.wait_recv()
            total = total + precv[c, k]
        out[c * (rows // SUB):(c + 1) * (rows // SUB)] = total

    for halo in halos:
        halo.wait_send()
    for swap in swaps:
        swap.wait_send()
    for _, push in pushes:
        push.wait_send()


def solution(mesh):
    groups = mesh.shape["gy"]

    def on_device(volume, sigma_fine, sigma_coarse):
        x_count, y_rows, z_count = volume.shape
        x_out, z_out = x_count // 2, z_count // 2
        lines = groups // PAIR
        tile = (x_out // CHUNKS // SUB, SUB, z_out)
        f32 = jnp.float32
        dma = pltpu.SemaphoreType.DMA
        smem = pl.BlockSpec(memory_space=pltpu.SMEM)
        result = pl.pallas_call(
            functools.partial(kernel, groups),
            out_shape=jax.ShapeDtypeStruct((x_out // SUB, SUB, z_out), f32),
            in_specs=[pl.BlockSpec(memory_space=pl.ANY), smem, smem],
            out_specs=pl.BlockSpec(memory_space=pltpu.VMEM),
            scratch_shapes=[
                pltpu.VMEM((y_rows, x_count, z_count), f32),
                pltpu.VMEM((y_rows, x_count, LANES), f32),
                pltpu.VMEM((2, x_out, x_count), f32),
                pltpu.VMEM((z_count + LANES, 2 * z_out), f32),
                pltpu.VMEM((2, x_count, y_rows * z_out), f32),
                pltpu.VMEM((CHUNKS, 2 * y_rows) + tile, f32),
                pltpu.VMEM((CHUNKS, 2 * y_rows) + tile, f32),
                pltpu.VMEM((CHUNKS, lines) + tile, f32),
                pltpu.VMEM((CHUNKS, lines) + tile, f32),
                dma((y_rows,)),
                dma((2, y_rows)),
                dma((CHUNKS,)),
                dma((CHUNKS,)),
                dma((CHUNKS, lines)),
                dma((CHUNKS, lines)),
            ],
            compiler_params=pltpu.CompilerParams(collective_id=0, has_side_effects=True),
        )(volume, sigma_fine, sigma_coarse)
        return result.reshape(x_out, 1, z_out)

    return jax.shard_map(
        on_device,
        mesh=mesh,
        in_specs=(P("parts", "gy", "gz"), P(), P()),
        out_specs=P("parts", "gy", "gz"),
        check_vma=False,
    )
```

time: 47.3 us -> 22.8 us (0.48)
  Pallas kernels: 0 us -> 21.2 us
  blocking collectives: 10.3 us -> 0 us
  starting transfers between devices: 10.3 us -> 0 us
  between operations: 7.74 us -> 0.01 us
  other arithmetic: 6.24 us -> 0 us
  waiting for transfers between devices: 5.61 us -> 0 us
  matrix products: 2.88 us -> 0 us
  local copies, waits for them, and re-layouts: 3.69 us -> 1.47 us
    pallas_call x0 -> x1, Pallas kernels: none -> 21.2 us  [on_device(): pl.pallas_call(functools.partial(kernel, groups), out_shape=jax.ShapeDtyp...]
    all_to_all x1 -> x0, blocking collectives: 10.3 us -> none  [on_device(): lax.all_to_all(columns[0] - columns[1], 'gy', split_axis=1, concat_axis=0...]
    all_to_all x1 -> x0, starting transfers between devices: 6.62 us -> none  [on_device(): lax.all_to_all(scaled, 'gy', split_axis=1, concat_axis=2, tiled=True)]
    all_to_all x1 -> x0, waiting for transfers between devices: 5.61 us -> none  [on_device(): lax.all_to_all(scaled, 'gy', split_axis=1, concat_axis=2, tiled=True)]
    select_n x3 -> x0, other arithmetic: 4.16 us -> none  [band_matrix(): mats.append(jnp.where(inside, values, jnp.float32(0.0)))]
    ppermute x2 -> x0, starting transfers between devices: 3.7 us -> none  [the longest x1 2.41 us: with_halo(): lax.ppermute(tail, axis, [(i, (i + 1) % count) for i in range(ends)])]
    dot_general x3 -> x0, matrix products: 2.88 us -> none  [the longest x1 1.66 us: on_device(): jnp.einsum('soi,iyz->soyz', matrix_x, volume, precision=lax.Precision.HIG...]
    reduce_sum x3 -> x0, other arithmetic: 2.05 us -> none  [band_matrix(): total = jnp.sum(jnp.exp(-offsets * offsets / (2.0 * sigma * sigma)))]
  transfers between devices with their start and end apart: 3 -> 0, of which waited for: 1 -> 0; matrix products, arithmetic and copies ran while one was open for 9% -> 0% of each run, Pallas kernels for 0% -> 0%
where the time goes in v1:
time: 22.8 us; the launch traced here: 22.6 us
  Pallas kernels  21.2 us (93%)
  local copies, waits for them, and re-layouts  1.47 us (6%)
    pallas_call x1, Pallas kernels, on_device(): pl.pallas_call(functools.partial(kernel, groups), out_shape=jax.ShapeDtyp...  21.2 us
    unnamed x1, local copies, waits for them, and re-layouts  1.47 us

profile of v1, /device:TPU:0, one launch (start us, length us, event | category | flops | bytes accessed | tf_op | source)
XLA Modules:
  0.0 22.6 jit_solution(10738619403934108745)
XLA Ops:
  0.0 21.2 %shard_map.37 = f32[16,8,128]{2,1,0:T(8,128)} custom-call(f32[256,2,256]{2,1,0:T(2,128)} %vol.1, f32[3]{0:T(128)} %sf.1, f32[3]{0:T(128)} %sc.1), custom_call_target="tpu_custom_call" | custom-call | tf_op jit(solution)/shard_map/pallas_call | solution.py:188
  21.2 1.5 %copy.6 = f32[128,1,128]{2,1,0:T(1,128)} copy(f32[128,1,128]{2,1,0:T(1,128)} %bitcast.3) | data formatting | bytes 131072

commit v2 on v1

--- a/solution.py
+++ b/solution.py
@@ -38,7 +38,7 @@
 
 
 def kernel(
-    groups, vol, sf, sc, out, vbuf, hbuf, wx, wz, zs, xsend, xrecv, psend, precv,
+    groups, vol, sf, sc, out, vbuf, wx, wz, zs, zh, hsend, hrecv, xsend, xrecv, psend, precv,
     load_sem, halo_sems, x_send_sems, x_recv_sems, p_send_sems, p_recv_sems,
 ):
     x_count, y_rows, z_count = vol.shape
@@ -65,29 +65,15 @@
     ]
     for load in loads:
         load.start()
-    pl.semaphore_wait(barrier, 1 + 1 + (lines - 1))
+
+    scales = [[tap_scale(ref[a]) for ref in (sf, sc)] for a in range(3)]
     edge = pl.multiple_of((1 - core) * (z_count - LANES), LANES)
-    halos = [
-        pltpu.make_async_remote_copy(
-            src_ref=vol.at[:, y, pl.ds(edge, LANES)],
-            dst_ref=hbuf.at[y],
-            send_sem=halo_sems.at[0, y],
-            recv_sem=halo_sems.at[1, y],
-            device_id={"gz": 1 - core},
-            device_id_type=MESH,
-        )
-        for y in range(y_rows)
-    ]
-    for halo in halos:
-        halo.start()
-
-    scales = [[tap_scale(ref[a]) for ref in (sf, sc)] for a in range(3)]
-    halo_first = z_count - (z_count + LANES) * core
+    edge_first = (z_count + LANES) * core - LANES
     for s in range(2):
         i = lax.broadcasted_iota(jnp.int32, (z_count, z_out), 0)
         o = lax.broadcasted_iota(jnp.int32, (z_count, z_out), 1)
         wz[:z_count, s * z_out:(s + 1) * z_out] = taps_at(i - 2 * o, scales[2][s])
-        i = lax.broadcasted_iota(jnp.int32, (LANES, z_out), 0) + halo_first
+        i = lax.broadcasted_iota(jnp.int32, (LANES, z_out), 0) + edge_first
         o = lax.broadcasted_iota(jnp.int32, (LANES, z_out), 1)
         wz[z_count:, s * z_out:(s + 1) * z_out] = taps_at(i - 2 * o, scales[2][s])
         for b in range(x_count // LANES):
@@ -98,19 +84,37 @@
     for y in range(y_rows):
         loads[y].wait()
         part = dot(vbuf[y], wz[:z_count, :])
-        halos[y].wait_recv()
-        part = part + dot(hbuf[y], wz[z_count:, :])
+        rim = dot(vbuf[y, :, pl.ds(edge, LANES)], wz[z_count:, :])
         for s in range(2):
             zs[s, :, y * z_out:(y + 1) * z_out] = part[:, s * z_out:(s + 1) * z_out]
+            zh[s, :, y * z_out:(y + 1) * z_out] = rim[:, s * z_out:(s + 1) * z_out]
+
+    for s in range(2):
+        for source, target in ((zs, xsend), (zh, hsend)):
+            part = dot(wx[s], source[s])
+            for y in range(y_rows):
+                target[:, s * y_rows + y] = part[:, y * z_out:(y + 1) * z_out].reshape(
+                    CHUNKS, rows // SUB, SUB, z_out
+                )
+
+    pl.semaphore_wait(barrier, 1 + 1 + (lines - 1))
+    halos = []
+    for c in range(CHUNKS):
+        halo = pltpu.make_async_remote_copy(
+            src_ref=hsend.at[c],
+            dst_ref=hrecv.at[c],
+            send_sem=halo_sems.at[0, c],
+            recv_sem=halo_sems.at[1, c],
+            device_id={"gz": 1 - core},
+            device_id_type=MESH,
+        )
+        halo.start()
+        halos.append(halo)
 
     swaps = []
     for c in range(CHUNKS):
-        for s in range(2):
-            part = dot(wx[s, c * rows:(c + 1) * rows, :], zs[s])
-            for y in range(y_rows):
-                xsend[c, s * y_rows + y] = part[:, y * z_out:(y + 1) * z_out].reshape(
-                    rows // SUB, SUB, z_out
-                )
+        halos[c].wait_recv()
+        xsend[c] = xsend[c] + hrecv[c]
         swap = pltpu.make_async_remote_copy(
             src_ref=xsend.at[c],
             dst_ref=xrecv.at[c],
@@ -122,6 +126,13 @@
         swap.start()
         swaps.append(swap)
 
+    def weighted(row_taps, held, c):
+        total = None
+        for j, tap in enumerate(row_taps):
+            term = tap * held[c, j]
+            total = term if total is None else total + term
+        return total
+
     def y_tap(s, row, target):
         d = jnp.full((SUB, LANES), row - 2 * target, jnp.int32)
         return taps_at(d, scales[1][s])[None]
@@ -138,14 +149,12 @@
     order = list(range(1, lines)) + [0]
     pushes = []
     for c in range(CHUNKS):
+        for k in order:
+            psend[c, k] = weighted(taps[k][0], xsend, c)
+    for c in range(CHUNKS):
         swaps[c].wait_recv()
         for k in order:
-            total = None
-            for held, row_taps in ((xsend, taps[k][0]), (xrecv, taps[k][1])):
-                for j, tap in enumerate(row_taps):
-                    term = tap * held[c, j]
-                    total = term if total is None else total + term
-            psend[c, k] = total
+            psend[c, k] = psend[c, k] + weighted(taps[k][1], xrecv, c)
             if k:
                 push = pltpu.make_async_remote_copy(
                     src_ref=psend.at[c, k],
@@ -192,16 +201,18 @@
             out_specs=pl.BlockSpec(memory_space=pltpu.VMEM),
             scratch_shapes=[
                 pltpu.VMEM((y_rows, x_count, z_count), f32),
-                pltpu.VMEM((y_rows, x_count, LANES), f32),
                 pltpu.VMEM((2, x_out, x_count), f32),
                 pltpu.VMEM((z_count + LANES, 2 * z_out), f32),
                 pltpu.VMEM((2, x_count, y_rows * z_out), f32),
+                pltpu.VMEM((2, x_count, y_rows * z_out), f32),
+                pltpu.VMEM((CHUNKS, 2 * y_rows) + tile, f32),
+                pltpu.VMEM((CHUNKS, 2 * y_rows) + tile, f32),
                 pltpu.VMEM((CHUNKS, 2 * y_rows) + tile, f32),
                 pltpu.VMEM((CHUNKS, 2 * y_rows) + tile, f32),
                 pltpu.VMEM((CHUNKS, lines) + tile, f32),
                 pltpu.VMEM((CHUNKS, lines) + tile, f32),
                 dma((y_rows,)),
-                dma((2, y_rows)),
+                dma((2, CHUNKS)),
                 dma((CHUNKS,)),
                 dma((CHUNKS,)),
                 dma((CHUNKS, lines)),

time: 22.8 us -> 22.3 us (0.978)
  Pallas kernels: 21.2 us -> 20.6 us
    pallas_call x1, Pallas kernels: 21.2 us -> 20.6 us  [on_device(): pl.pallas_call(functools.partial(kernel, groups), out_shape=jax.ShapeDtyp...]
where the time goes in v2:
time: 22.3 us; the launch traced here: 22.1 us
  Pallas kernels  20.6 us (92%)
  local copies, waits for them, and re-layouts  1.47 us (7%)
    pallas_call x1, Pallas kernels, on_device(): pl.pallas_call(functools.partial(kernel, groups), out_shape=jax.ShapeDtyp...  20.6 us
    unnamed x1, local copies, waits for them, and re-layouts  1.47 us

profile of v2, /device:TPU:0, one launch (start us, length us, event | category | flops | bytes accessed | tf_op | source)
XLA Modules:
  0.0 22.1 jit_solution(14289265635930803003)
XLA Ops:
  0.0 20.6 %shard_map.37 = f32[16,8,128]{2,1,0:T(8,128)} custom-call(f32[256,2,256]{2,1,0:T(2,128)} %vol.1, f32[3]{0:T(128)} %sf.1, f32[3]{0:T(128)} %sc.1), custom_call_target="tpu_custom_call" | custom-call | tf_op jit(solution)/shard_map/pallas_call | solution.py:197
  20.6 1.5 %copy.6 = f32[128,1,128]{2,1,0:T(1,128)} copy(f32[128,1,128]{2,1,0:T(1,128)} %bitcast.3) | data formatting | bytes 131072

commit v3 on v2

--- a/solution.py
+++ b/solution.py
@@ -11,12 +11,26 @@
 LANES = 128
 SUB = 8
 CHUNKS = 4
+RIM = 16
 PAIR = 2
 MESH = pl.DeviceIdType.MESH
 
 
-def dot(a, b):
-    return jnp.dot(a, b, precision=lax.Precision.HIGHEST, preferred_element_type=jnp.float32)
+def halves(value):
+    high = value.astype(jnp.bfloat16)
+    return high, (value - high.astype(jnp.float32)).astype(jnp.bfloat16)
+
+
+def dot(a, b, dim):
+    def term(p, q):
+        return lax.dot_general(p, q, (((1,), (dim,)), ((), ())), preferred_element_type=jnp.float32)
+
+    return term(a[0], b[0]) + (term(a[0], b[1]) + term(a[1], b[0]))
+
+
+def put(ref, place, value):
+    for index, half in enumerate(halves(value)):
+        ref[(index,) + place] = half
 
 
 def splat(value):
@@ -38,12 +52,12 @@
 
 
 def kernel(
-    groups, vol, sf, sc, out, vbuf, wx, wz, zs, zh, hsend, hrecv, xsend, xrecv, psend, precv,
+    groups, vol, sf, sc, out, vbuf, wx, wz, we, zs, zh, hsend, hrecv, xsend, xrecv, psend, precv, whole,
     load_sem, halo_sems, x_send_sems, x_recv_sems, p_send_sems, p_recv_sems,
 ):
     x_count, y_rows, z_count = vol.shape
     x_out, z_out = x_count // 2, z_count // 2
-    rows = x_out // CHUNKS
+    rows = z_out // CHUNKS
     lines = groups // PAIR
     me = lax.axis_index("gy")
     core = lax.axis_index("gz")
@@ -69,54 +83,59 @@
     scales = [[tap_scale(ref[a]) for ref in (sf, sc)] for a in range(3)]
     edge = pl.multiple_of((1 - core) * (z_count - LANES), LANES)
     edge_first = (z_count + LANES) * core - LANES
+    rim_first = (z_out - RIM) * core
     for s in range(2):
-        i = lax.broadcasted_iota(jnp.int32, (z_count, z_out), 0)
-        o = lax.broadcasted_iota(jnp.int32, (z_count, z_out), 1)
-        wz[:z_count, s * z_out:(s + 1) * z_out] = taps_at(i - 2 * o, scales[2][s])
-        i = lax.broadcasted_iota(jnp.int32, (LANES, z_out), 0) + edge_first
-        o = lax.broadcasted_iota(jnp.int32, (LANES, z_out), 1)
-        wz[z_count:, s * z_out:(s + 1) * z_out] = taps_at(i - 2 * o, scales[2][s])
-        for b in range(x_count // LANES):
-            o = lax.broadcasted_iota(jnp.int32, (x_out, LANES), 0)
-            i = lax.broadcasted_iota(jnp.int32, (x_out, LANES), 1) + b * LANES
-            wx[s, :, b * LANES:(b + 1) * LANES] = taps_at(i - 2 * o, scales[0][s])
+        for b in range(z_count // LANES):
+            o = lax.broadcasted_iota(jnp.int32, (z_out, LANES), 0)
+            i = lax.broadcasted_iota(jnp.int32, (z_out, LANES), 1) + b * LANES
+            place = (slice(s * z_out, (s + 1) * z_out), slice(b * LANES, (b + 1) * LANES))
+            put(wz, place, taps_at(i - 2 * o, scales[2][s]))
+        o = lax.broadcasted_iota(jnp.int32, (RIM, LANES), 0) + rim_first
+        i = lax.broadcasted_iota(jnp.int32, (RIM, LANES), 1) + edge_first
+        put(we, (slice(s * RIM, (s + 1) * RIM),), taps_at(i - 2 * o, scales[2][s]))
+        i = lax.broadcasted_iota(jnp.int32, (x_count, x_out), 0)
+        o = lax.broadcasted_iota(jnp.int32, (x_count, x_out), 1)
+        put(wx, (s,), taps_at(i - 2 * o, scales[0][s]))
 
     for y in range(y_rows):
         loads[y].wait()
-        part = dot(vbuf[y], wz[:z_count, :])
-        rim = dot(vbuf[y, :, pl.ds(edge, LANES)], wz[z_count:, :])
+        part = dot((wz[0], wz[1]), halves(vbuf[y]), 1)
+        rim = dot((we[0], we[1]), halves(vbuf[y, :, pl.ds(edge, LANES)]), 1)
         for s in range(2):
-            zs[s, :, y * z_out:(y + 1) * z_out] = part[:, s * z_out:(s + 1) * z_out]
-            zh[s, :, y * z_out:(y + 1) * z_out] = rim[:, s * z_out:(s + 1) * z_out]
+            put(zs, (s, slice(y * z_out, (y + 1) * z_out)), part[s * z_out:(s + 1) * z_out])
+            put(zh, (s, slice(y * RIM, (y + 1) * RIM)), rim[s * RIM:(s + 1) * RIM])
 
     for s in range(2):
-        for source, target in ((zs, xsend), (zh, hsend)):
-            part = dot(wx[s], source[s])
-            for y in range(y_rows):
-                target[:, s * y_rows + y] = part[:, y * z_out:(y + 1) * z_out].reshape(
-                    CHUNKS, rows // SUB, SUB, z_out
-                )
+        part = dot((zs[0, s], zs[1, s]), (wx[0, s], wx[1, s]), 0)
+        rim = dot((zh[0, s], zh[1, s]), (wx[0, s], wx[1, s]), 0)
+        for y in range(y_rows):
+            xsend[:, s * y_rows + y] = part[y * z_out:(y + 1) * z_out].reshape(
+                CHUNKS, rows // SUB, SUB, x_out
+            )
+            hsend[s * y_rows + y] = rim[y * RIM:(y + 1) * RIM].reshape(RIM // SUB, SUB, x_out)
 
     pl.semaphore_wait(barrier, 1 + 1 + (lines - 1))
-    halos = []
-    for c in range(CHUNKS):
-        halo = pltpu.make_async_remote_copy(
-            src_ref=hsend.at[c],
-            dst_ref=hrecv.at[c],
-            send_sem=halo_sems.at[0, c],
-            recv_sem=halo_sems.at[1, c],
-            device_id={"gz": 1 - core},
-            device_id_type=MESH,
-        )
-        halo.start()
-        halos.append(halo)
-
+    halo = pltpu.make_async_remote_copy(
+        src_ref=hsend,
+        dst_ref=hrecv,
+        send_sem=halo_sems.at[0],
+        recv_sem=halo_sems.at[1],
+        device_id={"gz": 1 - core},
+        device_id_type=MESH,
+    )
+    halo.start()
+
+    blocks = [c + (CHUNKS - 1 - 2 * c) * core for c in range(CHUNKS)]
+    rim_at = (1 - core) * (rows - RIM) // SUB
     swaps = []
     for c in range(CHUNKS):
-        halos[c].wait_recv()
-        xsend[c] = xsend[c] + hrecv[c]
+        if c == CHUNKS - 1:
+            halo.wait_recv()
+            for j in range(2 * y_rows):
+                place = (blocks[c], j, pl.ds(rim_at, RIM // SUB))
+                xsend[place] = xsend[place] + hrecv[j]
         swap = pltpu.make_async_remote_copy(
-            src_ref=xsend.at[c],
+            src_ref=xsend.at[blocks[c]],
             dst_ref=xrecv.at[c],
             send_sem=x_send_sems.at[c],
             recv_sem=x_recv_sems.at[c],
@@ -150,7 +169,7 @@
     pushes = []
     for c in range(CHUNKS):
         for k in order:
-            psend[c, k] = weighted(taps[k][0], xsend, c)
+            psend[c, k] = weighted(taps[k][0], xsend, blocks[c])
     for c in range(CHUNKS):
         swaps[c].wait_recv()
         for k in order:
@@ -173,10 +192,10 @@
         for k, push in enumerate(mine, start=1):
             push.wait_recv()
             total = total + precv[c, k]
-        out[c * (rows // SUB):(c + 1) * (rows // SUB)] = total
-
-    for halo in halos:
-        halo.wait_send()
+        whole[pl.ds(pl.multiple_of(blocks[c] * rows, rows), rows), :] = total.reshape(rows, x_out)
+
+    out[...] = whole[...].T.reshape(x_out // SUB, SUB, z_out)
+    halo.wait_send()
     for swap in swaps:
         swap.wait_send()
     for _, push in pushes:
@@ -190,7 +209,8 @@
         x_count, y_rows, z_count = volume.shape
         x_out, z_out = x_count // 2, z_count // 2
         lines = groups // PAIR
-        tile = (x_out // CHUNKS // SUB, SUB, z_out)
+        tile = (z_out // CHUNKS // SUB, SUB, x_out)
+        b16 = jnp.bfloat16
         f32 = jnp.float32
         dma = pltpu.SemaphoreType.DMA
         smem = pl.BlockSpec(memory_space=pltpu.SMEM)
@@ -201,18 +221,20 @@
             out_specs=pl.BlockSpec(memory_space=pltpu.VMEM),
             scratch_shapes=[
                 pltpu.VMEM((y_rows, x_count, z_count), f32),
-                pltpu.VMEM((2, x_out, x_count), f32),
-                pltpu.VMEM((z_count + LANES, 2 * z_out), f32),
-                pltpu.VMEM((2, x_count, y_rows * z_out), f32),
-                pltpu.VMEM((2, x_count, y_rows * z_out), f32),
-                pltpu.VMEM((CHUNKS, 2 * y_rows) + tile, f32),
-                pltpu.VMEM((CHUNKS, 2 * y_rows) + tile, f32),
+                pltpu.VMEM((2, 2, x_count, x_out), b16),
+                pltpu.VMEM((2, 2 * z_out, z_count), b16),
+                pltpu.VMEM((2, 2 * RIM, LANES), b16),
+                pltpu.VMEM((2, 2, y_rows * z_out, x_count), b16),
+                pltpu.VMEM((2, 2, y_rows * RIM, x_count), b16),
+                pltpu.VMEM((2 * y_rows, RIM // SUB, SUB, x_out), f32),
+                pltpu.VMEM((2 * y_rows, RIM // SUB, SUB, x_out), f32),
                 pltpu.VMEM((CHUNKS, 2 * y_rows) + tile, f32),
                 pltpu.VMEM((CHUNKS, 2 * y_rows) + tile, f32),
                 pltpu.VMEM((CHUNKS, lines) + tile, f32),
                 pltpu.VMEM((CHUNKS, lines) + tile, f32),
+                pltpu.VMEM((z_out, x_out), f32),
                 dma((y_rows,)),
-                dma((2, CHUNKS)),
+                dma((2,)),
                 dma((CHUNKS,)),
                 dma((CHUNKS,)),
                 dma((CHUNKS, lines)),

time: 22.3 us -> 20.2 us (0.906)
  Pallas kernels: 20.6 us -> 18.5 us
    pallas_call x1, Pallas kernels: 20.6 us -> 18.5 us  [on_device(): pl.pallas_call(functools.partial(kernel, groups), out_shape=jax.ShapeDtyp...]
where the time goes in v3:
time: 20.2 us; the launch traced here: 20 us
  Pallas kernels  18.5 us (92%)
  local copies, waits for them, and re-layouts  1.47 us (7%)
    pallas_call x1, Pallas kernels, on_device(): pl.pallas_call(functools.partial(kernel, groups), out_shape=jax.ShapeDtyp...  18.5 us
    unnamed x1, local copies, waits for them, and re-layouts  1.47 us

profile of v3, /device:TPU:0, one launch (start us, length us, event | category | flops | bytes accessed | tf_op | source)
XLA Modules:
  0.0 20.0 jit_solution(10326604811076771325)
XLA Ops:
  0.0 18.5 %shard_map.37 = f32[16,8,128]{2,1,0:T(8,128)} custom-call(f32[256,2,256]{2,1,0:T(2,128)} %vol.1, f32[3]{0:T(128)} %sf.1, f32[3]{0:T(128)} %sc.1), custom_call_target="tpu_custom_call" | custom-call | tf_op jit(solution)/shard_map/pallas_call | solution.py:217
  18.5 1.5 %copy.6 = f32[128,1,128]{2,1,0:T(1,128)} copy(f32[128,1,128]{2,1,0:T(1,128)} %bitcast.3) | data formatting | bytes 131072
